TPU v7x, 32 devices: a whole 2x2x4 slice. The times are simulated.
32 devices in a mesh: vocab: 8 (over y, x, core), blk: 4 (over z).
Axes of the slice: x: 2, y: 2, z: 4, core: 2. Of those that a mesh axis runs over, the one named last changes fastest.
Arguments:
- char_ids: int32 [16384, 50], P(('vocab', 'blk')), may hold values from 0 to 255, as said below
- char_table: bfloat16 [256, 16], replicated, may hold values from -5 to 5
- conv_weight: bfloat16 [112, 896], replicated, may hold values from -0.75 to 0.75
- proj_weight: bfloat16 [896, 1024], replicated, may hold values from -0.1875 to 0.1875
- gate_weight: bfloat16 [2, 1024, 1024], replicated, may hold values from -0.1875 to 0.1875
- trans_weight: bfloat16 [2, 1024, 1024], replicated, may hold values from -0.1875 to 0.1875
- gate_bias: float32 [2, 1024], replicated, may hold values from -4 to 4
- hidden: bfloat16 [2048, 1024], P(('vocab', 'blk')), may hold values from -48 to 48
- targets: int32 [2048], P(('vocab', 'blk')), may hold values from 0 to 16383
Outputs:
- row_loss: float32 [2048], P(('vocab', 'blk'))
- hidden_grad: bfloat16 [2048, 1024], P(('vocab', 'blk'))
Inputs may be any that keep to these rules, and one draw needn't show every extreme that they name: `char_ids`: each word has 2 to 50 characters with ids 1 and up, followed by the padding id 0.
All inputs are finite; a program needn't handle non-finite values.
Results may differ from a plain program's by a relative error of at most 0.014.
The roundings to bfloat16 on the way count: a program that leaves them out, or rounds other values in their place, can miss the bound.
Values may be sent and summed in bfloat16 or wider, within the bound.
No kernel may reach another device: no remote copies, remote signals or barrier semaphores. Data moves between devices by JAX's collectives and lax.ppermute only.
A program may use at most 128 MiB of HBM per device.

v0:
```python
import math
import jax
import jax.numpy as jnp
from jax import lax
from jax.sharding import PartitionSpec as P


def shifted(array, axis, by):
    count = lax.axis_size(axis)
    return lax.ppermute(array, axis, [(i, (i + by) % count) for i in range(count)])


def char_features(char_ids, char_table, conv_weight):
    num_words = char_ids.shape[0]
    length = char_ids.shape[1]
    symbols = char_table.shape[0]
    embed_dim = char_table.shape[1]
    widths = conv_weight.shape[0] // embed_dim
    filters = conv_weight.shape[1] // widths
    onehot = (char_ids[:, :, None] == jnp.arange(symbols, dtype=jnp.int32)[None, None, :]).astype(
        jnp.bfloat16
    )
    vectors = jnp.dot(
        onehot.reshape(num_words * length, symbols), char_table, preferred_element_type=jnp.float32
    )
    vectors = vectors.astype(jnp.bfloat16).reshape(num_words, length, embed_dim)
    padded = jnp.pad(vectors, ((0, 0), (0, widths - 1), (0, 0)))
    windows = jnp.concatenate(
        [padded[:, shift_at : shift_at + length, :] for shift_at in range(widths)], axis=2
    )
    offset = jnp.arange(widths * embed_dim) // embed_dim
    kernel = jnp.arange(widths * filters) // filters + 1
    masked = jnp.where(offset[:, None] < kernel[None, :], conv_weight, jnp.zeros_like(conv_weight))
    conv_out = jnp.dot(
        windows.reshape(num_words * length, widths * embed_dim),
        masked,
        preferred_element_type=jnp.float32,
    )
    conv_out = conv_out.reshape(num_words, length, widths * filters)
    position = jnp.arange(length)
    usable = position[:, None] <= length - kernel[None, :]
    pooled = jnp.max(jnp.where(usable[None, :, :], conv_out, -jnp.inf), axis=1)
    return jnp.tanh(pooled).astype(jnp.bfloat16)


def embed_words(
    char_ids, char_table, conv_weight, proj_weight, gate_weight, trans_weight, gate_bias
):
    features = char_features(char_ids, char_table, conv_weight)
    current = jnp.dot(features, proj_weight, preferred_element_type=jnp.float32).astype(
        jnp.bfloat16
    )
    for layer_idx in range(gate_weight.shape[0]):
        opened = jax.nn.sigmoid(
            jnp.dot(current, gate_weight[layer_idx], preferred_element_type=jnp.float32)
            + gate_bias[layer_idx]
        )
        carried = jax.nn.relu(
            jnp.dot(current, trans_weight[layer_idx], preferred_element_type=jnp.float32)
        )
        current = (opened * carried + (1.0 - opened) * current.astype(jnp.float32)).astype(
            jnp.bfloat16
        )
    return current


def embed_all(char_ids, char_table, conv_weight, proj_weight, gate_weight, trans_weight, gate_bias):
    num_total = char_ids.shape[0]
    block_size = math.gcd(num_total, 128)
    grouped = char_ids.reshape(num_total // block_size, block_size, char_ids.shape[1])

    def one_block(piece_ids):
        return embed_words(
            piece_ids, char_table, conv_weight, proj_weight, gate_weight, trans_weight, gate_bias
        )

    return lax.map(one_block, grouped).reshape(num_total, proj_weight.shape[1])


def pick_targets(word_panel, row_spot):
    count_words = word_panel.shape[0]
    inside = (row_spot >= 0) & (row_spot < count_words)
    picked = jnp.take(word_panel, jnp.clip(row_spot, 0, count_words - 1), axis=0).astype(
        jnp.float32
    )
    return jnp.where(inside[:, None], picked, jnp.zeros_like(picked))


def fold_panel(acc_state, row_block, row_spot, word_panel):
    run_max, run_total, weighted, target_vec = acc_state
    scores = lax.dot_general(
        row_block, word_panel, (((1,), (1,)), ((), ())), preferred_element_type=jnp.float32
    )
    new_max = jnp.maximum(run_max, jnp.max(scores, axis=1))
    rescale = jnp.exp(run_max - new_max)
    soft_weights = jnp.exp(scores - new_max[:, None]).astype(jnp.bfloat16)
    run_total = run_total * rescale + jnp.sum(soft_weights.astype(jnp.float32), axis=1)
    weighted = weighted * rescale[:, None] + jnp.dot(
        soft_weights, word_panel, preferred_element_type=jnp.float32
    )
    target_vec = target_vec + pick_targets(word_panel, row_spot)
    return (new_max, run_total, weighted, target_vec)


def finish_rows(hidden, run_max, run_total, weighted, target_vec):
    target_score = jnp.sum(hidden.astype(jnp.float32) * target_vec, axis=1)
    row_loss = run_max + jnp.log(run_total) - target_score
    hidden_grad = (weighted / run_total[:, None] - target_vec).astype(jnp.bfloat16)
    return (row_loss, hidden_grad)


def per_device(
    char_ids,
    char_table,
    conv_weight,
    proj_weight,
    gate_weight,
    trans_weight,
    gate_bias,
    hidden,
    targets,
):
    embeds = embed_all(
        char_ids, char_table, conv_weight, proj_weight, gate_weight, trans_weight, gate_bias
    )
    local_words = embeds.shape[0]
    my_rows = hidden.shape[0]
    model_dim = hidden.shape[1]
    blocks = lax.axis_size("blk")
    group_idx = lax.axis_index("blk")
    word_panel = lax.all_gather(embeds, "vocab", axis=0, tiled=True)
    group_hidden = lax.all_gather(hidden, "blk", axis=0, tiled=True)
    group_goal = lax.all_gather(targets, "blk", axis=0, tiled=True)
    owner_dev = group_goal // local_words
    in_group = owner_dev % blocks == group_idx
    spot_all = jnp.where(in_group, owner_dev // blocks * local_words + group_goal % local_words, -1)
    running = (
        jnp.full((my_rows,), -jnp.inf, jnp.float32),
        jnp.zeros((my_rows,), jnp.float32),
        jnp.zeros((my_rows, model_dim), jnp.float32),
        jnp.zeros((my_rows, model_dim), jnp.float32),
    )
    for step_idx in range(blocks):
        which_block = (group_idx - step_idx) % blocks
        row_block = lax.dynamic_slice_in_dim(group_hidden, which_block * my_rows, my_rows, 0)
        row_spot = lax.dynamic_slice_in_dim(spot_all, which_block * my_rows, my_rows, 0)
        running = fold_panel(running, row_block, row_spot, word_panel)
        running = shifted((running[0], running[1], running[2], running[3]), "blk", 1)
    run_max, run_total, weighted, target_vec = running
    return finish_rows(hidden, run_max, run_total, weighted, target_vec)


def solution(mesh):
    return jax.shard_map(
        per_device,
        mesh=mesh,
        in_specs=(
            P(("vocab", "blk"), None),
            P(),
            P(),
            P(),
            P(),
            P(),
            P(),
            P(("vocab", "blk"), None),
            P(("vocab", "blk")),
        ),
        out_specs=(P(("vocab", "blk")), P(("vocab", "blk"), None)),
        check_vma=False,
    )
```

profile of v0, /device:TPU:0, one launch (start us, length us, event | category | flops | bytes accessed | tf_op | source)
XLA Modules:
  0.0 273.5 jit_solution(3712595097836582395)
XLA Ops:
  8.3 100.8 %while.13 = (s32[]{:T(128)}, bf16[4,128,1024]{2,1,0:T(8,128)(2,1)}, s32[4,128,50]{2,1,0:T(8,128)S(1)}, bf16[256,16]{0,1:T(8,128)(2,1)}, bf16[112,896]{1,0:T(8,12...) while((s32[]{:T(128)}, bf16[4,128,1024]{2,1,0:T(8,128)(2,1)}, ...), condition=%wide.region_2.3_spmd, body=%wide.region_0.2_spmd.sunk | while | flops 2662044928 | bytes 67010176 | solution.py:77
  8.5 4.2 %convolution_convert_fusion.4 = bf16[6400,16]{0,1:T(8,128)(2,1)S(1)} fusion(bf16[256,16]{0,1:T(8,128)(2,1)} %get-tuple-element.308, s32[6400]{0:T(1024)S(1)} %eq.53), kind=kOutput, calls=%fused_computation.5.clone.1 | convolution fusion | flops 54169600 | bytes 238592 | tf_op jit(solution)/shard_map/while/body/eval_jaxpr/dot_general | solution.py:23
  24.2 4.8 %select_reduce_fusion.2 = f32[128,896]{1,0:T(8,128)S(1)} fusion(pred[50,896]{1,0:T(8,128)(4,1)S(1)} %iota_compare_fusion.6, bf16[128,50,112]{0,2,1:T(8,128)(2,1)} %constant_dynamic-update-slice_fusion.20, bf16[112,896]{1,0:T(8,128)(2,1)S(1)} %copy-done.9, s32[896]{0:T(1024)S(1)} %fusion.150, s32[112]{0:T(128)S(1)} %and_select_fusion.6), kind=kOutput, calls=%fused_computation.4.clone.1 | convolution fusion | flops 1296060416 | bytes 2141888 | tf_op jit(solution)/shard_map/while/body/eval_jaxpr/dot_general | solution.py:34
  33.7 4.2 %convolution_convert_fusion.4 = bf16[6400,16]{0,1:T(8,128)(2,1)S(1)} fusion(bf16[256,16]{0,1:T(8,128)(2,1)} %get-tuple-element.308, s32[6400]{0:T(1024)S(1)} %eq.53), kind=kOutput, calls=%fused_computation.5.clone.1 | convolution fusion | flops 54169600 | bytes 238592 | tf_op jit(solution)/shard_map/while/body/eval_jaxpr/dot_general | solution.py:23
  49.4 4.8 %select_reduce_fusion.2 = f32[128,896]{1,0:T(8,128)S(1)} fusion(pred[50,896]{1,0:T(8,128)(4,1)S(1)} %iota_compare_fusion.6, bf16[128,50,112]{0,2,1:T(8,128)(2,1)} %constant_dynamic-update-slice_fusion.20, bf16[112,896]{1,0:T(8,128)(2,1)S(1)} %copy-done.9, s32[896]{0:T(1024)S(1)} %fusion.150, s32[112]{0:T(128)S(1)} %and_select_fusion.6), kind=kOutput, calls=%fused_computation.4.clone.1 | convolution fusion | flops 1296060416 | bytes 2141888 | tf_op jit(solution)/shard_map/while/body/eval_jaxpr/dot_general | solution.py:34
  58.9 4.2 %convolution_convert_fusion.4 = bf16[6400,16]{0,1:T(8,128)(2,1)S(1)} fusion(bf16[256,16]{0,1:T(8,128)(2,1)} %get-tuple-element.308, s32[6400]{0:T(1024)S(1)} %eq.53), kind=kOutput, calls=%fused_computation.5.clone.1 | convolution fusion | flops 54169600 | bytes 238592 | tf_op jit(solution)/shard_map/while/body/eval_jaxpr/dot_general | solution.py:23
  74.6 4.8 %select_reduce_fusion.2 = f32[128,896]{1,0:T(8,128)S(1)} fusion(pred[50,896]{1,0:T(8,128)(4,1)S(1)} %iota_compare_fusion.6, bf16[128,50,112]{0,2,1:T(8,128)(2,1)} %constant_dynamic-update-slice_fusion.20, bf16[112,896]{1,0:T(8,128)(2,1)S(1)} %copy-done.9, s32[896]{0:T(1024)S(1)} %fusion.150, s32[112]{0:T(128)S(1)} %and_select_fusion.6), kind=kOutput, calls=%fused_computation.4.clone.1 | convolution fusion | flops 1296060416 | bytes 2141888 | tf_op jit(solution)/shard_map/while/body/eval_jaxpr/dot_general | solution.py:34
  84.1 4.2 %convolution_convert_fusion.4 = bf16[6400,16]{0,1:T(8,128)(2,1)S(1)} fusion(bf16[256,16]{0,1:T(8,128)(2,1)} %get-tuple-element.308, s32[6400]{0:T(1024)S(1)} %eq.53), kind=kOutput, calls=%fused_computation.5.clone.1 | convolution fusion | flops 54169600 | bytes 238592 | tf_op jit(solution)/shard_map/while/body/eval_jaxpr/dot_general | solution.py:23
  99.8 4.8 %select_reduce_fusion.2 = f32[128,896]{1,0:T(8,128)S(1)} fusion(pred[50,896]{1,0:T(8,128)(4,1)S(1)} %iota_compare_fusion.6, bf16[128,50,112]{0,2,1:T(8,128)(2,1)} %constant_dynamic-update-slice_fusion.20, bf16[112,896]{1,0:T(8,128)(2,1)S(1)} %copy-done.9, s32[896]{0:T(1024)S(1)} %fusion.150, s32[112]{0:T(128)S(1)} %and_select_fusion.6), kind=kOutput, calls=%fused_computation.4.clone.1 | convolution fusion | flops 1296060416 | bytes 2141888 | tf_op jit(solution)/shard_map/while/body/eval_jaxpr/dot_general | solution.py:34
  110.7 9.9 %all-reduce.1 = s32[256]{0:T(256)S(1)} all-reduce(s32[256]{0:T(256)S(1)} %dynamic-update-slice), channel_id=1, replica_groups=mesh['vocab'=8,'blk'=4] {'blk'}, use_global_device_ids=true, to_apply=%add.1 | all-reduce | flops 256 | bytes 2048
  121.3 15.9 %all_gather.9 = bf16[256,1024]{1,0:T(8,128)(2,1)S(1)} all-gather(bf16[64,1024]{1,0:T(8,128)(2,1)} %param.20), channel_id=1, replica_groups=mesh['vocab'=8,'blk'=4] {'blk'}, dimensions={0}, use_global_device_ids=true | all-gather | bytes 655360 | tf_op jit(solution)/shard_map/all_gather | solution.py:132
  137.3 29.1 %all-gather.2.cloned.1.call-done = bf16[4096,1024]{1,0:T(8,128)(2,1)} async-done(((bf16[512,1024]{1,0:T(8,128)(2,1)}), bf16[4096,1024]{1,0:T(8,128)(2,1)}) %all-gather.2.cloned.1.call-update) | async-done | bytes 8388624 | tf_op jit(solution)/shard_map/all_gather | solution.py:131
  166.3 5.3 %gather_fusion = bf16[64,1024]{1,0:T(8,128)(2,1)S(1)} fusion(bf16[4096,1024]{1,0:T(8,128)(2,1)} %all-gather.2.cloned.1.call-done, s32[1024]{0:T(1024)S(1)} %pad_clamp_fusion.3), kind=kCustom, calls=%fused_computation.clone | custom fusion | bytes 262400 | tf_op jit(solution)/shard_map/jit(_take)/gather | solution.py:83
  173.9 6.7 %fusion.101 = (f32[64]{0:T(128)S(1)}, f32[64,4096]{1,0:T(8,128)S(1)}) fusion(bf16[4096,1024]{1,0:T(8,128)(2,1)} %all-gather.2.cloned.1.call-done, bf16[256,1024]{1,0:T(8,128)(2,1)S(1)} %all_gather.9, s32[]{:T(128)S(6)} %select_n.128), kind=kOutput, calls=%fused_computation.147 | convolution fusion | flops 537132992 | bytes 9568516 | tf_op jit(solution)/shard_map/dot_general | solution.py:91
  187.1 3.3 %fusion.102 = (f32[64]{0:T(128)}, f32[64,4096]{1,0:T(8,128)S(1)}) fusion(bf16[4096,1024]{1,0:T(8,128)(2,1)S(1)} %copy-done, bf16[256,1024]{1,0:T(8,128)(2,1)S(1)} %all_gather.9, s32[]{:T(128)S(6)} %select_n.130), kind=kOutput, calls=%fused_computation.148 | convolution fusion | flops 537132992 | bytes 9568516 | tf_op jit(solution)/shard_map/dot_general | solution.py:91
  193.6 4.2 %fusion.104 = (f32[64]{0:T(128)}, f32[64,4096]{1,0:T(8,128)S(1)}) fusion(bf16[4096,1024]{1,0:T(8,128)(2,1)S(1)} %copy-done, bf16[256,1024]{1,0:T(8,128)(2,1)} %copy-done.2, s32[]{:T(128)S(6)} %select_n.134), kind=kOutput, calls=%fused_computation.150 | convolution fusion | flops 537132992 | bytes 9568516 | tf_op jit(solution)/shard_map/dot_general | solution.py:91
  197.8 5.3 %gather_fusion.1 = bf16[64,1024]{1,0:T(8,128)(2,1)S(1)} fusion(bf16[4096,1024]{1,0:T(8,128)(2,1)} %all-gather.2.cloned.1.call-done, s32[1024]{0:T(1024)S(1)} %pad_clamp_fusion.2), kind=kCustom, calls=%fused_computation.1.clone | custom fusion | bytes 262400 | tf_op jit(solution)/shard_map/jit(_take)/gather | solution.py:83
  203.0 5.3 %gather_fusion.2 = bf16[64,1024]{1,0:T(8,128)(2,1)S(1)} fusion(bf16[4096,1024]{1,0:T(8,128)(2,1)} %all-gather.2.cloned.1.call-done, s32[1024]{0:T(1024)S(1)} %pad_clamp_fusion.1), kind=kCustom, calls=%fused_computation.2.clone | custom fusion | bytes 262400 | tf_op jit(solution)/shard_map/jit(_take)/gather | solution.py:83
  208.3 5.3 %gather_fusion.3 = bf16[64,1024]{1,0:T(8,128)(2,1)S(1)} fusion(bf16[4096,1024]{1,0:T(8,128)(2,1)} %all-gather.2.cloned.1.call-done, s32[1024]{0:T(1024)S(1)} %pad_clamp_fusion), kind=kCustom, calls=%fused_computation.3.clone | custom fusion | bytes 262400 | tf_op jit(solution)/shard_map/jit(_take)/gather | solution.py:83
  227.5 5.2 %multiply_add_fusion.2 = f32[64,1024]{1,0:T(8,128)S(1)} fusion(f32[64,1024]{1,0:T(8,128)} %collective-permute-done.12, f32[64]{0:T(128)S(1)} %get-tuple-element.173, bf16[4096,1024]{1,0:T(8,128)(2,1)} %all-gather.2.cloned.1.call-done, f32[64,4096]{1,0:T(8,128)S(1)} %get-tuple-element.209, f32[64]{0:T(128)S(1)} %max.43), kind=kOutput, calls=%fused_computation.88 | convolution fusion | flops 537526272 | bytes 9961984 | tf_op jit(solution)/shard_map/dot_general | solution.py:98
  233.0 4.1 %collective-permute-done.9 = f32[64,1024]{1,0:T(8,128)S(1)} collective-permute-done((f32[64,1024]{1,0:T(8,128)S(1)}, f32[64,1024]{1,0:T(8,128)S(1)}, u32[]{:S(2)}, u32[]{:S(2)}) %collective-permute-start.9) | collective-permute-done | bytes 262176 | tf_op jit(solution)/shard_map/ppermute | solution.py:10
  237.3 6.5 %collective-permute-done.13 = f32[64,1024]{1,0:T(8,128)S(1)} collective-permute-done((f32[64,1024]{1,0:T(8,128)S(1)}, f32[64,1024]{1,0:T(8,128)S(1)}, u32[]{:S(2)}, u32[]{:S(2)}) %collective-permute-start.13) | collective-permute-done | bytes 262176 | tf_op jit(solution)/shard_map/ppermute | solution.py:10
  248.8 6.4 %collective-permute-done.14 = f32[64,1024]{1,0:T(8,128)S(1)} collective-permute-done((f32[64,1024]{1,0:T(8,128)S(1)}, f32[64,1024]{1,0:T(8,128)S(1)}, u32[]{:S(2)}, u32[]{:S(2)}) %collective-permute-start.14) | collective-permute-done | bytes 262176 | tf_op jit(solution)/shard_map/ppermute | solution.py:10
  259.7 5.6 %collective-permute-done.7 = f32[64]{0:T(128)S(1)} collective-permute-done((f32[64]{0:T(128)S(1)}, f32[64]{0:T(128)S(1)}, u32[]{:S(2)}, u32[]{:S(2)}) %collective-permute-start.7) | collective-permute-done | bytes 288 | tf_op jit(solution)/shard_map/ppermute | solution.py:10
  (233 shorter events, 104.1 us)
Async XLA Ops:
  7.2 159.2 %all-gather.2.cloned.1.call-start = ((), (), s32[]{:S(2)}) async-start(), calls=%async_computation | async-start | bytes 9437184 | tf_op jit(solution)/shard_map/all_gather | solution.py:131
  8.2 100.9 %copy-start.11 = (u32[32]{0:T(128)S(1)}, u32[32]{0:T(128)}, u32[]{:S(2)}) copy-start(u32[32]{0:T(128)} %constant.224) | copy-start | bytes 388
  8.3 102.2 %copy-start.10 = (s32[64]{0:T(128)S(1)}, s32[64]{0:T(128)}, u32[]{:S(2)}) copy-start(s32[64]{0:T(128)} %param.21) | copy-start | bytes 772
  137.3 53.1 %copy-start.2 = (bf16[256,1024]{1,0:T(8,128)(2,1)}, bf16[256,1024]{1,0:T(8,128)(2,1)S(1)}, u32[]{:S(2)}) copy-start(bf16[256,1024]{1,0:T(8,128)(2,1)S(1)} %all_gather.9) | copy-start | bytes 1572868
  172.4 10.7 %copy-start = (bf16[4096,1024]{1,0:T(8,128)(2,1)S(1)}, bf16[4096,1024]{1,0:T(8,128)(2,1)}, u32[]{:S(2)}) copy-start(bf16[4096,1024]{1,0:T(8,128)(2,1)} %all-gather.2.cloned.1.call-done) | copy-start | bytes 25165828
  172.4 53.7 %collective-permute-start.8 = (f32[64,1024]{1,0:T(8,128)}, f32[64,1024]{1,0:T(8,128)}, u32[]{:S(2)}, u32[]{:S(2)}) collective-permute-start(f32[64,1024]{1,0:T(8,128)} %convert_select_fusion), channel_id=1, source_target_pairs={{0,1},{1,2},{2,3},{3,0},{4,5},{5,6},{6,7},{7,4},{8,9},{9,10},{10,1... | collective-permute-start | bytes 786440 | tf_op jit(solution)/shard_map/ppermute | solution.py:10
  180.6 32.9 %collective-permute-start = (f32[64]{0:T(128)S(1)}, f32[64]{0:T(128)}, u32[]{:S(2)}, u32[]{:S(2)}) collective-permute-start(f32[64]{0:T(128)S(1)} %get-tuple-element.206), channel_id=1, source_target_pairs={{0,1},{1,2},{2,3},{3,0},{4,5},{5,6},{6,7},{7,4},{8,9},{9,10},{10,1... | collective-permute-start | bytes 776 | tf_op jit(solution)/shard_map/ppermute | solution.py:10
  185.5 41.9 %collective-permute-start.12 = (f32[64,1024]{1,0:T(8,128)}, f32[64,1024]{1,0:T(8,128)}, u32[]{:S(2)}, u32[]{:S(2)}) collective-permute-start(f32[64,1024]{1,0:T(8,128)} %convolution_add_fusion), channel_id=1, source_target_pairs={{0,1},{1,2},{2,3},{3,0},{4,5},{5,6},{6,7},{7,4},{8,9},{9,10},{10,1... | collective-permute-start | bytes 786440 | tf_op jit(solution)/shard_map/ppermute | solution.py:10
  187.0 29.4 %collective-permute-start.4 = (f32[64]{0:T(128)}, f32[64]{0:T(128)}, u32[]{:S(2)}, u32[]{:S(2)}) collective-permute-start(f32[64]{0:T(128)} %get-tuple-element.205), channel_id=1, source_target_pairs={{0,1},{1,2},{2,3},{3,0},{4,5},{5,6},{6,7},{7,4},{8,9},{9,10},{10,1... | collective-permute-start | bytes 776 | tf_op jit(solution)/shard_map/ppermute | solution.py:10
  214.2 5.3 %collective-permute-start.1 = (f32[64]{0:T(128)S(1)}, f32[64]{0:T(128)S(1)}, u32[]{:S(2)}, u32[]{:S(2)}) collective-permute-start(f32[64]{0:T(128)S(1)} %max.43), channel_id=1, source_target_pairs={{0,1},{1,2},{2,3},{3,0},{4,5},{5,6},{6,7},{7,4},{8,9},{9,10},{10,1... | collective-permute-start | bytes 776 | tf_op jit(solution)/shard_map/ppermute | solution.py:10
  217.0 5.3 %collective-permute-start.5 = (f32[64]{0:T(128)S(1)}, f32[64]{0:T(128)S(1)}, u32[]{:S(2)}, u32[]{:S(2)}) collective-permute-start(f32[64]{0:T(128)S(1)} %get-tuple-element.172), channel_id=1, source_target_pairs={{0,1},{1,2},{2,3},{3,0},{4,5},{5,6},{6,7},{7,4},{8,9},{9,10},{10,1... | collective-permute-start | bytes 776 | tf_op jit(solution)/shard_map/ppermute | solution.py:10
  220.2 5.3 %collective-permute-start.2 = (f32[64]{0:T(128)S(1)}, f32[64]{0:T(128)S(1)}, u32[]{:S(2)}, u32[]{:S(2)}) collective-permute-start(f32[64]{0:T(128)S(1)} %max.44), channel_id=1, source_target_pairs={{0,1},{1,2},{2,3},{3,0},{4,5},{5,6},{6,7},{7,4},{8,9},{9,10},{10,1... | collective-permute-start | bytes 776 | tf_op jit(solution)/shard_map/ppermute | solution.py:10
  220.6 23.1 %slice-start = ((s8[8388608]{0:T(1024)(128)(4,1)}), s8[4194304]{0:T(1024)(128)(4,1)S(1)}, s32[]{:S(2)}) async-start(s8[8388608]{0:T(1024)(128)(4,1)} %bitcast.111), calls=%async_computation.1 | async-start | bytes 8388608
  222.4 23.1 %collective-permute-start.6 = (f32[64]{0:T(128)S(1)}, f32[64]{0:T(128)S(1)}, u32[]{:S(2)}, u32[]{:S(2)}) collective-permute-start(f32[64]{0:T(128)S(1)} %get-tuple-element.170), channel_id=1, source_target_pairs={{0,1},{1,2},{2,3},{3,0},{4,5},{5,6},{6,7},{7,4},{8,9},{9,10},{10,1... | collective-permute-start | bytes 776 | tf_op jit(solution)/shard_map/ppermute | solution.py:10
  227.1 10.0 %collective-permute-start.9 = (f32[64,1024]{1,0:T(8,128)S(1)}, f32[64,1024]{1,0:T(8,128)S(1)}, u32[]{:S(2)}, u32[]{:S(2)}) collective-permute-start(f32[64,1024]{1,0:T(8,128)S(1)} %select_add_fusion.2), channel_id=1, source_target_pairs={{0,1},{1,2},{2,3},{3,0},{4,5},{5,6},{6,7},{7,4},{8,9},{9,10},{10,1... | collective-permute-start | bytes 786440 | tf_op jit(solution)/shard_map/ppermute | solution.py:10
  227.5 16.3 %slice-start.1 = ((s8[8388608]{0:T(1024)(128)(4,1)}), s8[4194304]{0:T(1024)(128)(4,1)S(1)}, s32[]{:S(2)}) async-start(s8[8388608]{0:T(1024)(128)(4,1)} %bitcast.111), calls=%async_computation.2 | async-start | bytes 8388608
  232.6 11.1 %collective-permute-start.13 = (f32[64,1024]{1,0:T(8,128)S(1)}, f32[64,1024]{1,0:T(8,128)S(1)}, u32[]{:S(2)}, u32[]{:S(2)}) collective-permute-start(f32[64,1024]{1,0:T(8,128)S(1)} %multiply_add_fusion.2), channel_id=1, source_target_pairs={{0,1},{1,2},{2,3},{3,0},{4,5},{5,6},{6,7},{7,4},{8,9},{9,10},{10,1... | collective-permute-start | bytes 786440 | tf_op jit(solution)/shard_map/ppermute | solution.py:10
  237.2 11.4 %collective-permute-start.10 = (f32[64,1024]{1,0:T(8,128)S(1)}, f32[64,1024]{1,0:T(8,128)S(1)}, u32[]{:S(2)}, u32[]{:S(2)}) collective-permute-start(f32[64,1024]{1,0:T(8,128)S(1)} %select_add_fusion.1), channel_id=1, source_target_pairs={{0,1},{1,2},{2,3},{3,0},{4,5},{5,6},{6,7},{7,4},{8,9},{9,10},{10,1... | collective-permute-start | bytes 786440 | tf_op jit(solution)/shard_map/ppermute | solution.py:10
  245.4 9.8 %collective-permute-start.14 = (f32[64,1024]{1,0:T(8,128)S(1)}, f32[64,1024]{1,0:T(8,128)S(1)}, u32[]{:S(2)}, u32[]{:S(2)}) collective-permute-start(f32[64,1024]{1,0:T(8,128)S(1)} %multiply_add_fusion.1), channel_id=1, source_target_pairs={{0,1},{1,2},{2,3},{3,0},{4,5},{5,6},{6,7},{7,4},{8,9},{9,10},{10,1... | collective-permute-start | bytes 786440 | tf_op jit(solution)/shard_map/ppermute | solution.py:10
  248.7 16.5 %collective-permute-start.11 = (f32[64,1024]{1,0:T(8,128)S(1)}, f32[64,1024]{1,0:T(8,128)S(1)}, u32[]{:S(2)}, u32[]{:S(2)}) collective-permute-start(f32[64,1024]{1,0:T(8,128)S(1)} %select_add_fusion), channel_id=1, source_target_pairs={{0,1},{1,2},{2,3},{3,0},{4,5},{5,6},{6,7},{7,4},{8,9},{9,10},{10,1... | collective-permute-start | bytes 786440 | tf_op jit(solution)/shard_map/ppermute | solution.py:10
  255.2 10.0 %copy-start.3 = (bf16[64,1024]{1,0:T(8,128)(2,1)S(1)}, bf16[64,1024]{1,0:T(8,128)(2,1)}, u32[]{:S(2)}) copy-start(bf16[64,1024]{1,0:T(8,128)(2,1)} %param.20) | copy-start | bytes 393220
  256.9 8.3 %collective-permute-start.15 = (f32[64,1024]{1,0:T(8,128)S(1)}, f32[64,1024]{1,0:T(8,128)S(1)}, u32[]{:S(2)}, u32[]{:S(2)}) collective-permute-start(f32[64,1024]{1,0:T(8,128)S(1)} %multiply_add_fusion), channel_id=1, source_target_pairs={{0,1},{1,2},{2,3},{3,0},{4,5},{5,6},{6,7},{7,4},{8,9},{9,10},{10,1... | collective-permute-start | bytes 786440 | tf_op jit(solution)/shard_map/ppermute | solution.py:10
  257.0 8.2 %collective-permute-start.7 = (f32[64]{0:T(128)S(1)}, f32[64]{0:T(128)S(1)}, u32[]{:S(2)}, u32[]{:S(2)}) collective-permute-start(f32[64]{0:T(128)S(1)} %get-tuple-element.168), channel_id=1, source_target_pairs={{0,1},{1,2},{2,3},{3,0},{4,5},{5,6},{6,7},{7,4},{8,9},{9,10},{10,1... | collective-permute-start | bytes 776 | tf_op jit(solution)/shard_map/ppermute | solution.py:10
  257.2 8.9 %collective-permute-start.3 = (f32[64]{0:T(128)S(1)}, f32[64]{0:T(128)S(1)}, u32[]{:S(2)}, u32[]{:S(2)}) collective-permute-start(f32[64]{0:T(128)S(1)} %max.45), channel_id=1, source_target_pairs={{0,1},{1,2},{2,3},{3,0},{4,5},{5,6},{6,7},{7,4},{8,9},{9,10},{10,1... | collective-permute-start | bytes 776 | tf_op jit(solution)/shard_map/ppermute | solution.py:10
  (22 other events, 119.4 us)
Sparse Core Ops, SparseCore 0:
  109.2 57.0 all-gather.1
where the time goes:
time: 274 us; the launch traced here: 273 us
  matrix products  77.2 us (28%)
  local copies, waits for them, and re-layouts  74.1 us (27%)
  waiting for transfers between devices  60.3 us (22%)
  blocking collectives  25.8 us (9%)
  between operations  15.1 us (6%)
  starting transfers between devices  11.7 us (4%)
  other arithmetic  8.73 us (3%)
    ppermute x16, waiting for transfers between devices, shifted(): lax.ppermute(array, axis, [(i, (i + by) % count) for i in range(count)])  31.2 us
    all_gather x1, waiting for transfers between devices, per_device(): word_panel = lax.all_gather(embeds, 'vocab', axis=0, tiled=True)  29.1 us
    while x64, local copies, waits for them, and re-layouts  22.6 us
    gather x4, local copies, waits for them, and re-layouts, pick_targets(): jnp.take(word_panel, jnp.clip(row_spot, 0, count_words - 1), axis=0)  21 us
    dot_general x4, matrix products, char_features(): jnp.dot(windows.reshape(num_words * length, widths * embed_dim), masked,...  19.3 us
    slice x28, local copies, waits for them, and re-layouts, char_features(): padded[:, shift_at:shift_at + length, :]  17.8 us
    dot_general x4, matrix products, fold_panel(): lax.dot_general(row_block, word_panel, (((1,), (1,)), ((), ())), preferre...  17.4 us
    dot_general x4, matrix products, char_features(): jnp.dot(onehot.reshape(num_words * length, symbols), char_table, preferre...  16.7 us
  transfers between devices with their start and end apart: 17, of which 9 were waited for; matrix products, arithmetic and copies ran while one was open for 19% of the time, Pallas kernels for 0%

commit v1 on v0

--- a/solution.py
+++ b/solution.py
@@ -128,7 +128,14 @@
     model_dim = hidden.shape[1]
     blocks = lax.axis_size("blk")
     group_idx = lax.axis_index("blk")
-    word_panel = lax.all_gather(embeds, "vocab", axis=0, tiled=True)
+    ring = [embeds]
+    for hop in range(7):
+        ring.append(lax.ppermute(ring[-1], "vocab", [(dev, (dev + 1) % 8) for dev in range(8)]))
+    word_panel = jnp.roll(
+        jnp.concatenate(ring[::-1], axis=0),
+        (lax.axis_index("vocab") + 1) * ring[0].shape[0],
+        axis=0,
+    )
     group_hidden = lax.all_gather(hidden, "blk", axis=0, tiled=True)
     group_goal = lax.all_gather(targets, "blk", axis=0, tiled=True)
     owner_dev = group_goal // local_words

time: 274 us -> 373 us (1.36)
  waiting for transfers between devices: 60.3 us -> 124 us
  local copies, waits for them, and re-layouts: 74.1 us -> 119 us
  between operations: 15.1 us -> 1.62 us
  matrix products: 77.2 us -> 82 us
    ppermute x0 -> x7, waiting for transfers between devices: none -> 91.3 us  [per_device(): lax.ppermute(ring[-1], 'vocab', [(dev, (dev + 1) % 8) for dev in range(8)])]
    all_gather x1 -> x0, waiting for transfers between devices: 29.1 us -> none  [per_device(): word_panel = lax.all_gather(embeds, 'vocab', axis=0, tiled=True)]
    unnamed x22 -> x47, local copies, waits for them, and re-layouts: 1.9 us -> 27.5 us
    dynamic_slice x0 -> x1, local copies, waits for them, and re-layouts: none -> 7.62 us  [per_device(): jnp.roll(jnp.concatenate(ring[::-1], axis=0), (lax.axis_index('vocab') +...]
    while x64 -> x72, local copies, waits for them, and re-layouts: 22.6 us -> 28.6 us
    slice x28, local copies, waits for them, and re-layouts: 17.8 us -> 23.2 us  [char_features(): padded[:, shift_at:shift_at + length, :]]
  transfers between devices with their start and end apart: 17 -> 23, of which waited for: 9 -> 15; matrix products, arithmetic and copies ran while one was open for 19% -> 11% of each run, Pallas kernels for 0% -> 0%
where the time goes in v1:
time: 373 us; the launch traced here: 372 us
  waiting for transfers between devices  124 us (33%)
  local copies, waits for them, and re-layouts  119 us (32%)
  matrix products  82 us (22%)
  blocking collectives  25 us (7%)
  other arithmetic  10 us (3%)
  starting transfers between devices  9.09 us (2%)
    ppermute x7, waiting for transfers between devices, per_device(): lax.ppermute(ring[-1], 'vocab', [(dev, (dev + 1) % 8) for dev in range(8)])  91.3 us
    ppermute x16, waiting for transfers between devices, shifted(): lax.ppermute(array, axis, [(i, (i + by) % count) for i in range(count)])  32.9 us
    while x72, local copies, waits for them, and re-layouts  28.6 us
    unnamed x47, local copies, waits for them, and re-layouts  27.5 us
    slice x28, local copies, waits for them, and re-layouts, char_features(): padded[:, shift_at:shift_at + length, :]  23.2 us
    gather x4, local copies, waits for them, and re-layouts, pick_targets(): jnp.take(word_panel, jnp.clip(row_spot, 0, count_words - 1), axis=0)  21 us
    dot_general x4, matrix products, char_features(): jnp.dot(windows.reshape(num_words * length, widths * embed_dim), masked,...  20.5 us
    dot_general x4, matrix products, fold_panel(): lax.dot_general(row_block, word_panel, (((1,), (1,)), ((), ())), preferre...  17.3 us
  transfers between devices with their start and end apart: 23, of which 15 were waited for; matrix products, arithmetic and copies ran while one was open for 11% of the time, Pallas kernels for 0%

profile of v1, /device:TPU:0, one launch (start us, length us, event | category | flops | bytes accessed | tf_op | source)
XLA Modules:
  0.0 371.9 jit_solution(16271750154902497822)
XLA Ops:
  1.7 113.2 %while.13 = (s32[]{:T(128)}, bf16[4,128,1024]{2,1,0:T(8,128)(2,1)}, s32[4,128,50]{2,1,0:T(8,128)S(1)}, bf16[256,16]{0,1:T(8,128)(2,1)}, bf16[112,896]{1,0:T(8,12...) while((s32[]{:T(128)}, bf16[4,128,1024]{2,1,0:T(8,128)(2,1)}, ...), condition=%wide.region_2.3_spmd, body=%wide.region_0.2_spmd.sunk | while | flops 2662044928 | bytes 67026588 | solution.py:77
  21.5 5.1 %select_reduce_fusion.2 = f32[128,896]{1,0:T(8,128)S(1)} fusion(pred[50,896]{1,0:T(8,128)(4,1)S(1)} %iota_compare_fusion.6, bf16[128,50,112]{0,2,1:T(8,128)(2,1)} %constant_dynamic-update-slice_fusion.36, bf16[112,896]{1,0:T(8,128)(2,1)} %get-tuple-element.309, s32[896]{0:T(1024)S(1)} %fusion.150, s32[112]{0:T(128)S(1)} %and_select_fusion.6), kind=kOutput, calls=%fused_computation.4.clone.1 | convolution fusion | flops 1296060416 | bytes 2141888 | tf_op jit(solution)/shard_map/while/body/eval_jaxpr/dot_general | solution.py:34
  49.8 5.1 %select_reduce_fusion.2 = f32[128,896]{1,0:T(8,128)S(1)} fusion(pred[50,896]{1,0:T(8,128)(4,1)S(1)} %iota_compare_fusion.6, bf16[128,50,112]{0,2,1:T(8,128)(2,1)} %constant_dynamic-update-slice_fusion.36, bf16[112,896]{1,0:T(8,128)(2,1)} %get-tuple-element.309, s32[896]{0:T(1024)S(1)} %fusion.150, s32[112]{0:T(128)S(1)} %and_select_fusion.6), kind=kOutput, calls=%fused_computation.4.clone.1 | convolution fusion | flops 1296060416 | bytes 2141888 | tf_op jit(solution)/shard_map/while/body/eval_jaxpr/dot_general | solution.py:34
  78.1 5.1 %select_reduce_fusion.2 = f32[128,896]{1,0:T(8,128)S(1)} fusion(pred[50,896]{1,0:T(8,128)(4,1)S(1)} %iota_compare_fusion.6, bf16[128,50,112]{0,2,1:T(8,128)(2,1)} %constant_dynamic-update-slice_fusion.36, bf16[112,896]{1,0:T(8,128)(2,1)} %get-tuple-element.309, s32[896]{0:T(1024)S(1)} %fusion.150, s32[112]{0:T(128)S(1)} %and_select_fusion.6), kind=kOutput, calls=%fused_computation.4.clone.1 | convolution fusion | flops 1296060416 | bytes 2141888 | tf_op jit(solution)/shard_map/while/body/eval_jaxpr/dot_general | solution.py:34
  106.4 5.1 %select_reduce_fusion.2 = f32[128,896]{1,0:T(8,128)S(1)} fusion(pred[50,896]{1,0:T(8,128)(4,1)S(1)} %iota_compare_fusion.6, bf16[128,50,112]{0,2,1:T(8,128)(2,1)} %constant_dynamic-update-slice_fusion.36, bf16[112,896]{1,0:T(8,128)(2,1)} %get-tuple-element.309, s32[896]{0:T(1024)S(1)} %fusion.150, s32[112]{0:T(128)S(1)} %and_select_fusion.6), kind=kOutput, calls=%fused_computation.4.clone.1 | convolution fusion | flops 1296060416 | bytes 2141888 | tf_op jit(solution)/shard_map/while/body/eval_jaxpr/dot_general | solution.py:34
  115.3 15.6 %collective-permute-done = bf16[512,1024]{1,0:T(8,128)(2,1)S(1)} collective-permute-done((bf16[512,1024]{1,0:T(8,128)(2,1)}, bf16[512,1024]{1,0:T(8,128)(2,1)S(1)}, u32[]{:S(2)}, u32[]{:S(2)}) %collective-permute-start) | collective-permute-done | bytes 1048608 | tf_op jit(solution)/shard_map/ppermute | solution.py:133
  130.9 15.1 %collective-permute-done.1 = bf16[512,1024]{1,0:T(8,128)(2,1)S(1)} collective-permute-done((bf16[512,1024]{1,0:T(8,128)(2,1)S(1)}, bf16[512,1024]{1,0:T(8,128)(2,1)S(1)}, u32[]{:S(2)}, u32[]{:S(2)}) %collective-permute-start.1) | collective-permute-done | bytes 1048608 | tf_op jit(solution)/shard_map/ppermute | solution.py:133
  146.0 15.1 %collective-permute-done.2 = bf16[512,1024]{1,0:T(8,128)(2,1)S(1)} collective-permute-done((bf16[512,1024]{1,0:T(8,128)(2,1)S(1)}, bf16[512,1024]{1,0:T(8,128)(2,1)S(1)}, u32[]{:S(2)}, u32[]{:S(2)}) %collective-permute-start.2) | collective-permute-done | bytes 1048608 | tf_op jit(solution)/shard_map/ppermute | solution.py:133
  161.1 15.1 %collective-permute-done.3 = bf16[512,1024]{1,0:T(8,128)(2,1)S(1)} collective-permute-done((bf16[512,1024]{1,0:T(8,128)(2,1)S(1)}, bf16[512,1024]{1,0:T(8,128)(2,1)S(1)}, u32[]{:S(2)}, u32[]{:S(2)}) %collective-permute-start.3) | collective-permute-done | bytes 1048608 | tf_op jit(solution)/shard_map/ppermute | solution.py:133
  177.3 15.1 %collective-permute-done.4 = bf16[512,1024]{1,0:T(8,128)(2,1)S(1)} collective-permute-done((bf16[512,1024]{1,0:T(8,128)(2,1)S(1)}, bf16[512,1024]{1,0:T(8,128)(2,1)S(1)}, u32[]{:S(2)}, u32[]{:S(2)}) %collective-permute-start.4) | collective-permute-done | bytes 1048608 | tf_op jit(solution)/shard_map/ppermute | solution.py:133
  193.4 15.2 %collective-permute-done.5 = bf16[512,1024]{1,0:T(8,128)(2,1)} collective-permute-done((bf16[512,1024]{1,0:T(8,128)(2,1)S(1)}, bf16[512,1024]{1,0:T(8,128)(2,1)}, u32[]{:S(2)}, u32[]{:S(2)}) %collective-permute-start.5) | collective-permute-done | bytes 1048608 | tf_op jit(solution)/shard_map/ppermute | solution.py:133
  210.1 9.2 %all-reduce.1 = s32[256]{0:T(256)S(1)} all-reduce(s32[256]{0:T(256)S(1)} %dynamic-update-slice), channel_id=1, replica_groups=mesh['vocab'=8,'blk'=4] {'blk'}, use_global_device_ids=true, to_apply=%add.1 | all-reduce | flops 256 | bytes 2048
  220.1 15.8 %all_gather.6 = bf16[256,1024]{1,0:T(8,128)(2,1)S(1)} all-gather(bf16[64,1024]{1,0:T(8,128)(2,1)} %param.20), channel_id=1, replica_groups=mesh['vocab'=8,'blk'=4] {'blk'}, dimensions={0}, use_global_device_ids=true | all-gather | bytes 655360 | tf_op jit(solution)/shard_map/all_gather | solution.py:139
  260.5 7.6 %constant_dynamic-slice_fusion.1 = bf16[4096,1024]{1,0:T(8,128)(2,1)} fusion(bf16[8192,1024]{1,0:T(8,128)(2,1)} %constant_dynamic-update-slice_fusion.7, s32[]{:T(128)S(6)} %select_n.142), kind=kLoop, calls=%fused_computation.148 | loop fusion | bytes 16777220 | tf_op jit(solution)/shard_map/jit(_roll_dynamic)/dynamic_slice | solution.py:134
  268.2 7.3 %fusion.101 = (f32[64]{0:T(128)S(1)}, f32[64,4096]{1,0:T(8,128)}) fusion(bf16[4096,1024]{1,0:T(8,128)(2,1)} %constant_dynamic-slice_fusion.1, bf16[256,1024]{1,0:T(8,128)(2,1)S(1)} %all_gather.6, s32[]{:T(128)S(6)} %select_n.140), kind=kOutput, calls=%fused_computation.164 | convolution fusion | flops 537132992 | bytes 9568516 | tf_op jit(solution)/shard_map/dot_general | solution.py:91
  285.4 5.3 %gather_fusion = bf16[64,1024]{1,0:T(8,128)(2,1)S(1)} fusion(bf16[4096,1024]{1,0:T(8,128)(2,1)} %constant_dynamic-slice_fusion.1, s32[1024]{0:T(1024)S(1)} %pad_clamp_fusion.3), kind=kCustom, calls=%fused_computation.clone | custom fusion | bytes 262400 | tf_op jit(solution)/shard_map/jit(_take)/gather | solution.py:83
  291.5 5.3 %gather_fusion.1 = bf16[64,1024]{1,0:T(8,128)(2,1)S(1)} fusion(bf16[4096,1024]{1,0:T(8,128)(2,1)} %constant_dynamic-slice_fusion.1, s32[1024]{0:T(1024)S(1)} %pad_clamp_fusion.2), kind=kCustom, calls=%fused_computation.1.clone | custom fusion | bytes 262400 | tf_op jit(solution)/shard_map/jit(_take)/gather | solution.py:83
  300.2 6.1 %convolution_add_fusion = f32[64,1024]{1,0:T(8,128)} fusion(bf16[4096,1024]{1,0:T(8,128)(2,1)} %constant_dynamic-slice_fusion.1, f32[64]{0:T(128)S(1)} %get-tuple-element.204, f32[64,4096]{1,0:T(8,128)} %get-tuple-element.207, f32[64]{0:T(128)S(1)} %get-tuple-element.206), kind=kOutput, calls=%fused_computation.76 | convolution fusion | flops 537460736 | bytes 9699840 | tf_op jit(solution)/shard_map/dot_general | solution.py:98
  306.3 5.3 %gather_fusion.2 = bf16[64,1024]{1,0:T(8,128)(2,1)S(1)} fusion(bf16[4096,1024]{1,0:T(8,128)(2,1)} %constant_dynamic-slice_fusion.1, s32[1024]{0:T(1024)S(1)} %pad_clamp_fusion.1), kind=kCustom, calls=%fused_computation.2.clone | custom fusion | bytes 262400 | tf_op jit(solution)/shard_map/jit(_take)/gather | solution.py:83
  311.5 5.3 %gather_fusion.3 = bf16[64,1024]{1,0:T(8,128)(2,1)S(1)} fusion(bf16[4096,1024]{1,0:T(8,128)(2,1)} %constant_dynamic-slice_fusion.1, s32[1024]{0:T(1024)S(1)} %pad_clamp_fusion), kind=kCustom, calls=%fused_computation.3.clone | custom fusion | bytes 262400 | tf_op jit(solution)/shard_map/jit(_take)/gather | solution.py:83
  334.3 5.2 %multiply_add_fusion.2 = f32[64,1024]{1,0:T(8,128)S(1)} fusion(f32[64,1024]{1,0:T(8,128)S(1)} %collective-permute-done.19, f32[64]{0:T(128)S(1)} %get-tuple-element.173, bf16[4096,1024]{1,0:T(8,128)(2,1)} %constant_dynamic-slice_fusion.1, f32[64,4096]{1,0:T(8,128)S(1)} %get-tuple-element.209, f32[64]{0:T(128)S(1)} %max.43), kind=kOutput, calls=%fused_computation.88 | convolution fusion | flops 537526272 | bytes 9961984 | tf_op jit(solution)/shard_map/dot_general | solution.py:98
  343.8 6.8 %collective-permute-done.20 = f32[64,1024]{1,0:T(8,128)S(1)} collective-permute-done((f32[64,1024]{1,0:T(8,128)S(1)}, f32[64,1024]{1,0:T(8,128)S(1)}, u32[]{:S(2)}, u32[]{:S(2)}) %collective-permute-start.20) | collective-permute-done | bytes 262176 | tf_op jit(solution)/shard_map/ppermute | solution.py:10
  355.7 4.8 %collective-permute-done.21 = f32[64,1024]{1,0:T(8,128)S(1)} collective-permute-done((f32[64,1024]{1,0:T(8,128)S(1)}, f32[64,1024]{1,0:T(8,128)S(1)}, u32[]{:S(2)}, u32[]{:S(2)}) %collective-permute-start.21) | collective-permute-done | bytes 262176 | tf_op jit(solution)/shard_map/ppermute | solution.py:10
  363.6 6.9 %collective-permute-done.14 = f32[64]{0:T(128)S(1)} collective-permute-done((f32[64]{0:T(128)S(1)}, f32[64]{0:T(128)S(1)}, u32[]{:S(2)}, u32[]{:S(2)}) %collective-permute-start.14) | collective-permute-done | bytes 288 | tf_op jit(solution)/shard_map/ppermute | solution.py:10
  (279 shorter events, 167.3 us)
Async XLA Ops:
  1.7 208.2 %copy-start.16 = (s32[64]{0:T(128)S(1)}, s32[64]{0:T(128)}, u32[]{:S(2)}) copy-start(s32[64]{0:T(128)} %param.21) | copy-start | bytes 772
  114.9 16.0 %collective-permute-start = (bf16[512,1024]{1,0:T(8,128)(2,1)}, bf16[512,1024]{1,0:T(8,128)(2,1)S(1)}, u32[]{:S(2)}, u32[]{:S(2)}) collective-permute-start(bf16[512,1024]{1,0:T(8,128)(2,1)} %bitcast.113), channel_id=1, source_target_pairs={{0,4},{4,8},{8,12},{12,16},{16,20},{20,24},{24,28},{28,0},{1,5},{5... | collective-permute-start | bytes 3145736 | tf_op jit(solution)/shard_map/ppermute | solution.py:133
  130.9 15.1 %collective-permute-start.1 = (bf16[512,1024]{1,0:T(8,128)(2,1)S(1)}, bf16[512,1024]{1,0:T(8,128)(2,1)S(1)}, u32[]{:S(2)}, u32[]{:S(2)}) collective-permute-start(bf16[512,1024]{1,0:T(8,128)(2,1)S(1)} %collective-permute-done), channel_id=1, source_target_pairs={{0,4},{4,8},{8,12},{12,16},{16,20},{20,24},{24,28},{28,0},{1,5},{5... | collective-permute-start | bytes 3145736 | tf_op jit(solution)/shard_map/ppermute | solution.py:133
  146.0 15.1 %collective-permute-start.2 = (bf16[512,1024]{1,0:T(8,128)(2,1)S(1)}, bf16[512,1024]{1,0:T(8,128)(2,1)S(1)}, u32[]{:S(2)}, u32[]{:S(2)}) collective-permute-start(bf16[512,1024]{1,0:T(8,128)(2,1)S(1)} %collective-permute-done.1), channel_id=1, source_target_pairs={{0,4},{4,8},{8,12},{12,16},{16,20},{20,24},{24,28},{28,0},{1,5},{5... | collective-permute-start | bytes 3145736 | tf_op jit(solution)/shard_map/ppermute | solution.py:133
  161.1 15.1 %collective-permute-start.3 = (bf16[512,1024]{1,0:T(8,128)(2,1)S(1)}, bf16[512,1024]{1,0:T(8,128)(2,1)S(1)}, u32[]{:S(2)}, u32[]{:S(2)}) collective-permute-start(bf16[512,1024]{1,0:T(8,128)(2,1)S(1)} %collective-permute-done.2), channel_id=1, source_target_pairs={{0,4},{4,8},{8,12},{12,16},{16,20},{20,24},{24,28},{28,0},{1,5},{5... | collective-permute-start | bytes 3145736 | tf_op jit(solution)/shard_map/ppermute | solution.py:133
  177.3 15.1 %collective-permute-start.4 = (bf16[512,1024]{1,0:T(8,128)(2,1)S(1)}, bf16[512,1024]{1,0:T(8,128)(2,1)S(1)}, u32[]{:S(2)}, u32[]{:S(2)}) collective-permute-start(bf16[512,1024]{1,0:T(8,128)(2,1)S(1)} %collective-permute-done.3), channel_id=1, source_target_pairs={{0,4},{4,8},{8,12},{12,16},{16,20},{20,24},{24,28},{28,0},{1,5},{5... | collective-permute-start | bytes 3145736 | tf_op jit(solution)/shard_map/ppermute | solution.py:133
  193.4 15.2 %collective-permute-start.5 = (bf16[512,1024]{1,0:T(8,128)(2,1)S(1)}, bf16[512,1024]{1,0:T(8,128)(2,1)}, u32[]{:S(2)}, u32[]{:S(2)}) collective-permute-start(bf16[512,1024]{1,0:T(8,128)(2,1)S(1)} %collective-permute-done.4), channel_id=1, source_target_pairs={{0,4},{4,8},{8,12},{12,16},{16,20},{20,24},{24,28},{28,0},{1,5},{5... | collective-permute-start | bytes 3145736 | tf_op jit(solution)/shard_map/ppermute | solution.py:133
  208.6 27.3 %collective-permute-start.6 = (bf16[512,1024]{1,0:T(8,128)(2,1)}, bf16[512,1024]{1,0:T(8,128)(2,1)}, u32[]{:S(2)}, u32[]{:S(2)}) collective-permute-start(bf16[512,1024]{1,0:T(8,128)(2,1)} %collective-permute-done.5), channel_id=1, source_target_pairs={{0,4},{4,8},{8,12},{12,16},{16,20},{20,24},{24,28},{28,0},{1,5},{5... | collective-permute-start | bytes 3145736 | tf_op jit(solution)/shard_map/ppermute | solution.py:133
  291.5 41.7 %collective-permute-start.15 = (f32[64,1024]{1,0:T(8,128)}, f32[64,1024]{1,0:T(8,128)}, u32[]{:S(2)}, u32[]{:S(2)}) collective-permute-start(f32[64,1024]{1,0:T(8,128)} %convert_select_fusion), channel_id=1, source_target_pairs={{0,1},{1,2},{2,3},{3,0},{4,5},{5,6},{6,7},{7,4},{8,9},{9,10},{10,1... | collective-permute-start | bytes 786440 | tf_op jit(solution)/shard_map/ppermute | solution.py:10
  296.8 23.7 %collective-permute-start.7 = (f32[64]{0:T(128)S(1)}, f32[64]{0:T(128)}, u32[]{:S(2)}, u32[]{:S(2)}) collective-permute-start(f32[64]{0:T(128)S(1)} %get-tuple-element.206), channel_id=1, source_target_pairs={{0,1},{1,2},{2,3},{3,0},{4,5},{5,6},{6,7},{7,4},{8,9},{9,10},{10,1... | collective-permute-start | bytes 776 | tf_op jit(solution)/shard_map/ppermute | solution.py:10
  316.8 17.5 %collective-permute-start.19 = (f32[64,1024]{1,0:T(8,128)}, f32[64,1024]{1,0:T(8,128)S(1)}, u32[]{:S(2)}, u32[]{:S(2)}) collective-permute-start(f32[64,1024]{1,0:T(8,128)} %convolution_add_fusion), channel_id=1, source_target_pairs={{0,1},{1,2},{2,3},{3,0},{4,5},{5,6},{6,7},{7,4},{8,9},{9,10},{10,1... | collective-permute-start | bytes 786440 | tf_op jit(solution)/shard_map/ppermute | solution.py:10
  318.4 6.9 %collective-permute-start.11 = (f32[64]{0:T(128)}, f32[64]{0:T(128)S(1)}, u32[]{:S(2)}, u32[]{:S(2)}) collective-permute-start(f32[64]{0:T(128)} %get-tuple-element.205), channel_id=1, source_target_pairs={{0,1},{1,2},{2,3},{3,0},{4,5},{5,6},{6,7},{7,4},{8,9},{9,10},{10,1... | collective-permute-start | bytes 776 | tf_op jit(solution)/shard_map/ppermute | solution.py:10
  321.2 5.3 %collective-permute-start.8 = (f32[64]{0:T(128)S(1)}, f32[64]{0:T(128)S(1)}, u32[]{:S(2)}, u32[]{:S(2)}) collective-permute-start(f32[64]{0:T(128)S(1)} %max.43), channel_id=1, source_target_pairs={{0,1},{1,2},{2,3},{3,0},{4,5},{5,6},{6,7},{7,4},{8,9},{9,10},{10,1... | collective-permute-start | bytes 776 | tf_op jit(solution)/shard_map/ppermute | solution.py:10
  325.9 5.3 %collective-permute-start.12 = (f32[64]{0:T(128)S(1)}, f32[64]{0:T(128)S(1)}, u32[]{:S(2)}, u32[]{:S(2)}) collective-permute-start(f32[64]{0:T(128)S(1)} %get-tuple-element.172), channel_id=1, source_target_pairs={{0,1},{1,2},{2,3},{3,0},{4,5},{5,6},{6,7},{7,4},{8,9},{9,10},{10,1... | collective-permute-start | bytes 776 | tf_op jit(solution)/shard_map/ppermute | solution.py:10
  327.2 5.3 %collective-permute-start.9 = (f32[64]{0:T(128)S(1)}, f32[64]{0:T(128)S(1)}, u32[]{:S(2)}, u32[]{:S(2)}) collective-permute-start(f32[64]{0:T(128)S(1)} %max.44), channel_id=1, source_target_pairs={{0,1},{1,2},{2,3},{3,0},{4,5},{5,6},{6,7},{7,4},{8,9},{9,10},{10,1... | collective-permute-start | bytes 776 | tf_op jit(solution)/shard_map/ppermute | solution.py:10
  331.2 21.2 %collective-permute-start.13 = (f32[64]{0:T(128)S(1)}, f32[64]{0:T(128)S(1)}, u32[]{:S(2)}, u32[]{:S(2)}) collective-permute-start(f32[64]{0:T(128)S(1)} %get-tuple-element.170), channel_id=1, source_target_pairs={{0,1},{1,2},{2,3},{3,0},{4,5},{5,6},{6,7},{7,4},{8,9},{9,10},{10,1... | collective-permute-start | bytes 776 | tf_op jit(solution)/shard_map/ppermute | solution.py:10
  334.2 9.4 %collective-permute-start.16 = (f32[64,1024]{1,0:T(8,128)S(1)}, f32[64,1024]{1,0:T(8,128)S(1)}, u32[]{:S(2)}, u32[]{:S(2)}) collective-permute-start(f32[64,1024]{1,0:T(8,128)S(1)} %select_add_fusion.2), channel_id=1, source_target_pairs={{0,1},{1,2},{2,3},{3,0},{4,5},{5,6},{6,7},{7,4},{8,9},{9,10},{10,1... | collective-permute-start | bytes 786440 | tf_op jit(solution)/shard_map/ppermute | solution.py:10
  339.5 11.1 %collective-permute-start.20 = (f32[64,1024]{1,0:T(8,128)S(1)}, f32[64,1024]{1,0:T(8,128)S(1)}, u32[]{:S(2)}, u32[]{:S(2)}) collective-permute-start(f32[64,1024]{1,0:T(8,128)S(1)} %multiply_add_fusion.2), channel_id=1, source_target_pairs={{0,1},{1,2},{2,3},{3,0},{4,5},{5,6},{6,7},{7,4},{8,9},{9,10},{10,1... | collective-permute-start | bytes 786440 | tf_op jit(solution)/shard_map/ppermute | solution.py:10
  343.8 11.8 %collective-permute-start.17 = (f32[64,1024]{1,0:T(8,128)S(1)}, f32[64,1024]{1,0:T(8,128)S(1)}, u32[]{:S(2)}, u32[]{:S(2)}) collective-permute-start(f32[64,1024]{1,0:T(8,128)S(1)} %select_add_fusion.1), channel_id=1, source_target_pairs={{0,1},{1,2},{2,3},{3,0},{4,5},{5,6},{6,7},{7,4},{8,9},{9,10},{10,1... | collective-permute-start | bytes 786440 | tf_op jit(solution)/shard_map/ppermute | solution.py:10
  352.3 8.2 %collective-permute-start.21 = (f32[64,1024]{1,0:T(8,128)S(1)}, f32[64,1024]{1,0:T(8,128)S(1)}, u32[]{:S(2)}, u32[]{:S(2)}) collective-permute-start(f32[64,1024]{1,0:T(8,128)S(1)} %multiply_add_fusion.1), channel_id=1, source_target_pairs={{0,1},{1,2},{2,3},{3,0},{4,5},{5,6},{6,7},{7,4},{8,9},{9,10},{10,1... | collective-permute-start | bytes 786440 | tf_op jit(solution)/shard_map/ppermute | solution.py:10
  355.6 14.9 %collective-permute-start.18 = (f32[64,1024]{1,0:T(8,128)S(1)}, f32[64,1024]{1,0:T(8,128)S(1)}, u32[]{:S(2)}, u32[]{:S(2)}) collective-permute-start(f32[64,1024]{1,0:T(8,128)S(1)} %select_add_fusion), channel_id=1, source_target_pairs={{0,1},{1,2},{2,3},{3,0},{4,5},{5,6},{6,7},{7,4},{8,9},{9,10},{10,1... | collective-permute-start | bytes 786440 | tf_op jit(solution)/shard_map/ppermute | solution.py:10
  362.3 8.3 %collective-permute-start.22 = (f32[64,1024]{1,0:T(8,128)S(1)}, f32[64,1024]{1,0:T(8,128)S(1)}, u32[]{:S(2)}, u32[]{:S(2)}) collective-permute-start(f32[64,1024]{1,0:T(8,128)S(1)} %multiply_add_fusion), channel_id=1, source_target_pairs={{0,1},{1,2},{2,3},{3,0},{4,5},{5,6},{6,7},{7,4},{8,9},{9,10},{10,1... | collective-permute-start | bytes 786440 | tf_op jit(solution)/shard_map/ppermute | solution.py:10
  362.3 8.2 %collective-permute-start.14 = (f32[64]{0:T(128)S(1)}, f32[64]{0:T(128)S(1)}, u32[]{:S(2)}, u32[]{:S(2)}) collective-permute-start(f32[64]{0:T(128)S(1)} %get-tuple-element.168), channel_id=1, source_target_pairs={{0,1},{1,2},{2,3},{3,0},{4,5},{5,6},{6,7},{7,4},{8,9},{9,10},{10,1... | collective-permute-start | bytes 776 | tf_op jit(solution)/shard_map/ppermute | solution.py:10
  362.4 9.0 %collective-permute-start.10 = (f32[64]{0:T(128)S(1)}, f32[64]{0:T(128)S(1)}, u32[]{:S(2)}, u32[]{:S(2)}) collective-permute-start(f32[64]{0:T(128)S(1)} %max.45), channel_id=1, source_target_pairs={{0,1},{1,2},{2,3},{3,0},{4,5},{5,6},{6,7},{7,4},{8,9},{9,10},{10,1... | collective-permute-start | bytes 776 | tf_op jit(solution)/shard_map/ppermute | solution.py:10
  (37 other events, 484.7 us)
